TPU v7x, 256 devices: a whole 4x4x8 slice. The times are simulated.
256 devices in a mesh: rows: 8 (over x, core), cols: 32 (over y, z).
Axes of the slice: x: 4, y: 4, z: 8, core: 2. Of those that a mesh axis runs over, the one named last changes fastest.
Arguments:
- features: bfloat16 [256, 4096, 1536], P('rows', 'cols'), may hold values from -6 to 6
- projection: bfloat16 [1536, 128], replicated, may hold values from -0.4375 to 0.4375
- prev_dist: float32 [256, 4096], P('rows', 'cols'), may hold values from 0.5 to 3
- valid: int32 [256, 4096], P('rows', 'cols'), may hold values 0 or 1
- pick_owner: int32 [512], replicated, may hold values from 0 to 255, as said below
- pick_slot: int32 [512], replicated, may hold values from 0 to 4095, as said below
Outputs:
- min_dist: float32 [256, 4096], P('rows', 'cols')
Inputs may be any that keep to these rules, and one draw needn't show every extreme that they name: `pick_owner`: no two picks name the same patch; picks fall on devices at random. `pick_slot`: see pick_owner.
All inputs are finite; a program needn't handle non-finite values. No bound on the sum of `valid` on one device may be relied on, other than what follows from the above.
Results may differ from a plain program's by a relative error of at most 0.0003.
Values may be sent and summed in bfloat16 or wider, within the bound.
A program may use at most 128 MiB of HBM per device.

v0:
```python
import jax
import jax.numpy as jnp
from jax import lax
from jax.sharding import PartitionSpec as P

D_PROJ = 128


def padded_2(block, sides, width):
    for axis, dim in sides:
        count = lax.axis_size(axis)
        forward = [(i, i + 1) for i in range(count - 1)]
        backward = [(target, source) for source, target in forward]
        low = lax.ppermute(
            lax.slice_in_dim(block, block.shape[dim] - width, None, axis=dim), axis, forward
        )
        high = lax.ppermute(lax.slice_in_dim(block, 0, width, axis=dim), axis, backward)
        block = jnp.concatenate([low, block, high], axis=dim)
    return block


def window_sum(padded, rows_dev, cols_dev):
    total = jnp.zeros((rows_dev, cols_dev, padded.shape[2]), jnp.float32)
    for row_off in range(3):
        for col_off in range(3):
            total = total + padded[
                row_off : row_off + rows_dev, col_off : col_off + cols_dev
            ].astype(jnp.float32)
    return total / 9.0


def shards(features, projection, prev_dist, valid, pick_owner, pick_slot):
    rows_dev, cols_dev, channels = features.shape
    proj_full = projection.astype(jnp.float32)
    own_index = lax.axis_index("rows") * lax.axis_size("cols") + lax.axis_index("cols")
    owned = pick_owner == own_index
    padded = padded_2(features, (("rows", 0), ("cols", 1)), 1)
    pooled = window_sum(padded, rows_dev, cols_dev).reshape(rows_dev * cols_dev, channels)
    projected = jnp.dot(pooled, proj_full, precision=lax.Precision.HIGHEST)
    local_rows = jnp.where(owned[:, None], projected[pick_slot], jnp.float32(0.0))
    pick_rows = lax.psum(local_rows, ("rows", "cols"))
    pick_sq = jnp.sum(pick_rows * pick_rows, axis=1)
    own_sq = jnp.sum(projected * projected, axis=1)
    inner_prod = jnp.dot(projected, pick_rows.T, precision=lax.Precision.HIGHEST)
    scaled_gap = (own_sq[:, None] + pick_sq[None, :] - 2.0 * inner_prod) / D_PROJ
    nearest = jnp.min(scaled_gap, axis=1).reshape(rows_dev, cols_dev)
    return jnp.where(valid == 1, jnp.minimum(prev_dist, nearest), jnp.float32(0.0))


def solution(mesh):
    return jax.shard_map(
        shards,
        mesh=mesh,
        in_specs=(P("rows", "cols", None), P(), P("rows", "cols"), P("rows", "cols"), P(), P()),
        out_specs=P("rows", "cols"),
        check_vma=False,
    )
```

profile of v0, /device:TPU:2, one launch (start us, length us, event | category | flops | bytes accessed | tf_op | source)
XLA Modules:
  0.0 382.1 jit_solution(17740806826330092399)
XLA Ops:
  6.5 0.0 copy-start
  6.5 0.0 all-reduce.2.cloned.1.call-start
  6.5 1.2 fusion.6
  7.8 1.9 collective-permute-start
  9.7 3.6 collective-permute-start.1
  13.3 0.7 broadcast_compare_fusion
  14.0 0.7 compare_select_fusion
  14.7 2.1 collective-permute-done
  16.9 6.7 %constant_dynamic-update-slice_fusion.1 = bf16[34,128,1536]{2,1,0:T(8,128)(2,1)S(1)} fusion(bf16[34,128,1536]{2,1,0:T(8,128)(2,1)S(1)} %constant_dynamic-update-slice_fusion.2, bf16[32,128,1536]{2,1,0:T(8,128)(2,1)} %param.6), kind=kLoop, calls=%fused_computation.25 | loop fusion | bytes 25165824
  23.6 0.0 collective-permute-done.1
  23.6 0.0 copy-start.1
  23.6 4.8 %copy-done.1 = bf16[34,128,1536]{2,1,0:T(8,128)(2,1)} copy-done((bf16[34,128,1536]{2,1,0:T(8,128)(2,1)}, bf16[34,128,1536]{2,1,0:T(8,128)(2,1)S(1)}, u32[]{:S(2)}) %copy-start.1) | copy-done | bytes 13369368
  28.5 0.3 fusion.5
  28.8 3.8 %collective-permute-start.2 = (bf16[34,1,1536]{2,0,1:T(8,128)(2,1)S(1)}, bf16[34,1,1536]{2,0,1:T(8,128)(2,1)S(1)}, u32[]{:S(2)}, u32[]{:S(2)}) collective-permute-start(bf16[34,1,1536]{2,0,1:T(8,128)(2,1)S(1)} %copy.15), channel_id=1, source_target_pairs={{0,1},{1,2},{2,3},{3,4},{4,5},{5,6},{6,7},{7,8},{8,9},{9,10},{10,1... | collective-permute-start | bytes 313352 | tf_op jit(solution)/shard_map/ppermute | solution.py:14
  32.7 1.3 collective-permute-start.3
  34.0 1.1 collective-permute-done.2
  35.1 0.2 copy.16
  35.2 4.2 %collective-permute-done.3 = bf16[34,1,1536]{2,0,1:T(8,128)(2,1)S(1)} collective-permute-done((bf16[34,1,1536]{2,0,1:T(8,128)(2,1)S(1)}, bf16[34,1,1536]{2,0,1:T(8,128)(2,1)S(1)}, u32[]{:S(2)}, u32[]{:S(2)}) %collective-permute-start.3) | collective-permute-done | bytes 104480 | tf_op jit(solution)/shard_map/ppermute | solution.py:17
  39.5 0.2 copy.18
  39.6 47.2 %add_multiply_fusion = f32[32,128,1536]{2,1,0:T(8,128)} fusion(bf16[32,128,1536]{2,1,0:T(8,128)(2,1)} %param.6, bf16[34,128,1536]{2,1,0:T(8,128)(2,1)} %copy-done.1, bf16[34,1,1536]{2,1,0:T(2,128)(2,1)S(1)} %copy.18, bf16[34,1,1536]{2,1,0:T(2,128)(2,1)S(1)} %copy.16, bf16[1,128,1536]{2,1,0:T(8,128)(2,1)S(1)} %collective-permute-done.1, ...), kind=kLoop, calls=%fused_computation.1 | loop fusion | flops 264241152 | bytes 52113408 | tf_op jit(solution)/shard_map/div | solution.py:29
  86.8 0.0 copy-done
  86.9 18.7 %multiply_reduce_fusion.1 = (f32[4096]{0:T(1024)S(1)}, f32[4096,128]{0,1:T(8,128)S(1)}) fusion(f32[4096,1536]{1,0:T(8,128)} %bitcast.9, bf16[1536,128]{1,0:T(8,128)(2,1)S(1)} %copy-done), kind=kOutput, calls=%fused_computation.19 | convolution fusion | flops 9664720896 | bytes 27672576 | tf_op jit(solution)/shard_map/dot_general | solution.py:39
  105.6 0.0 copy-start.2
  105.6 0.0 copy-start.3
  105.6 1.9 copy.19
  107.5 2.6 gather_fusion
  110.1 0.8 broadcast_select_fusion
  111.0 0.0 all-reduce.2.cloned.1.call-update
  111.0 253.3 %all-reduce.2.cloned.1.call-done = f32[512,128]{1,0:T(8,128)} async-done(((f32[512,128]{1,0:T(8,128)}), f32[512,128]{1,0:T(8,128)}) %all-reduce.2.cloned.1.call-update) | async-done | bytes 262160 | tf_op jit(solution)/shard_map/psum | solution.py:41
  364.3 1.1 multiply_reduce_fusion.2
  365.4 9.2 %multiply_reduce_fusion = f32[4096]{0:T(1024)S(1)} fusion(f32[4096,128]{0,1:T(8,128)S(1)} %get-tuple-element.10, f32[512,128]{1,0:T(8,128)} %all-reduce.2.cloned.1.call-done, f32[512]{0:T(512)S(1)} %multiply_reduce_fusion.2, f32[4096]{0:T(1024)S(1)} %get-tuple-element.9), kind=kOutput, calls=%fused_computation.18 | convolution fusion | flops 3231707136 | bytes 2394112 | tf_op jit(solution)/shard_map/dot_general | solution.py:44
  374.7 0.6 fusion.4
  (7 shorter events, 0.1 us)
Async XLA Ops:
  6.5 80.3 %copy-start = (bf16[1536,128]{1,0:T(8,128)(2,1)S(1)}, bf16[1536,128]{1,0:T(8,128)(2,1)}, u32[]{:S(2)}) copy-start(bf16[1536,128]{1,0:T(8,128)(2,1)} %param.7) | copy-start | bytes 1179652
  6.5 357.8 %all-reduce.2.cloned.1.call-start = ((), (), s32[]{:S(2)}) async-start(), calls=%async_computation | async-start | bytes 524288 | tf_op jit(solution)/shard_map/psum | solution.py:41
  7.8 9.1 %collective-permute-start = (bf16[1,128,1536]{2,1,0:T(8,128)(2,1)S(1)}, bf16[1,128,1536]{2,1,0:T(8,128)(2,1)S(1)}, u32[]{:S(2)}, u32[]{:S(2)}) collective-permute-start(bf16[1,128,1536]{2,1,0:T(8,128)(2,1)S(1)} %get-tuple-element.8), channel_id=1, source_target_pairs={{0,32},{32,64},{64,96},{96,128},{128,160},{160,192},{192,224},{1,3... | collective-permute-start | bytes 1179656 | tf_op jit(solution)/shard_map/ppermute | solution.py:14
  9.7 13.9 %collective-permute-start.1 = (bf16[1,128,1536]{2,1,0:T(8,128)(2,1)S(1)}, bf16[1,128,1536]{2,1,0:T(8,128)(2,1)S(1)}, u32[]{:S(2)}, u32[]{:S(2)}) collective-permute-start(bf16[1,128,1536]{2,1,0:T(8,128)(2,1)S(1)} %get-tuple-element.7), channel_id=1, source_target_pairs={{32,0},{64,32},{96,64},{128,96},{160,128},{192,160},{224,192},{33,... | collective-permute-start | bytes 1179656 | tf_op jit(solution)/shard_map/ppermute | solution.py:17
  23.6 4.8 %copy-start.1 = (bf16[34,128,1536]{2,1,0:T(8,128)(2,1)}, bf16[34,128,1536]{2,1,0:T(8,128)(2,1)S(1)}, u32[]{:S(2)}) copy-start(bf16[34,128,1536]{2,1,0:T(8,128)(2,1)S(1)} %constant_dynamic-update-slice_fusion) | copy-start | bytes 40108036
  28.8 6.3 %collective-permute-start.2 = (bf16[34,1,1536]{2,0,1:T(8,128)(2,1)S(1)}, bf16[34,1,1536]{2,0,1:T(8,128)(2,1)S(1)}, u32[]{:S(2)}, u32[]{:S(2)}) collective-permute-start(bf16[34,1,1536]{2,0,1:T(8,128)(2,1)S(1)} %copy.15), channel_id=1, source_target_pairs={{0,1},{1,2},{2,3},{3,4},{4,5},{5,6},{6,7},{7,8},{8,9},{9,10},{10,1... | collective-permute-start | bytes 313352 | tf_op jit(solution)/shard_map/ppermute | solution.py:14
  32.7 6.8 %collective-permute-start.3 = (bf16[34,1,1536]{2,0,1:T(8,128)(2,1)S(1)}, bf16[34,1,1536]{2,0,1:T(8,128)(2,1)S(1)}, u32[]{:S(2)}, u32[]{:S(2)}) collective-permute-start(bf16[34,1,1536]{2,0,1:T(8,128)(2,1)S(1)} %copy.17), channel_id=1, source_target_pairs={{1,0},{2,1},{3,2},{4,3},{5,4},{6,5},{7,6},{8,7},{9,8},{10,9},{11,1... | collective-permute-start | bytes 313352 | tf_op jit(solution)/shard_map/ppermute | solution.py:17
  105.6 269.0 %copy-start.2 = (f32[32,128]{1,0:T(8,128)S(1)}, f32[32,128]{1,0:T(8,128)}, u32[]{:S(2)}) copy-start(f32[32,128]{1,0:T(8,128)} %param.8) | copy-start | bytes 49156
  105.6 269.0 %copy-start.3 = (s32[32,128]{1,0:T(8,128)S(1)}, s32[32,128]{1,0:T(8,128)}, u32[]{:S(2)}) copy-start(s32[32,128]{1,0:T(8,128)} %param.9) | copy-start | bytes 49156
Sparse Core Ops, SparseCore 0:
  111.1 253.1 all-reduce.1
where the time goes:
time: 382 us
  waiting for transfers between devices  261 us (68%)
  other arithmetic  51.2 us (13%)
  matrix products  27.9 us (7%)
  local copies, waits for them, and re-layouts  18 us (5%)
  between operations  13.6 us (4%)
  starting transfers between devices  10.7 us (3%)
    psum x1, waiting for transfers between devices, shards(): pick_rows = lax.psum(local_rows, ('rows', 'cols'))  253 us
    div x1, other arithmetic, window_sum(): return total / 9.0  47.2 us
    dot_general x1, matrix products, shards(): projected = jnp.dot(pooled, proj_full, precision=lax.Precision.HIGHEST)  18.7 us
    unnamed x10, local copies, waits for them, and re-layouts  11.6 us
    dot_general x1, matrix products, shards(): jnp.dot(projected, pick_rows.T, precision=lax.Precision.HIGHEST)  9.21 us
  transfers between devices with their start and end apart: 5, of which 4 were waited for; matrix products, arithmetic and copies ran while one was open for 2% of the time, Pallas kernels for 0%

commit v1 on v0

--- a/solution.py
+++ b/solution.py
@@ -38,7 +38,8 @@
     pooled = window_sum(padded, rows_dev, cols_dev).reshape(rows_dev * cols_dev, channels)
     projected = jnp.dot(pooled, proj_full, precision=lax.Precision.HIGHEST)
     local_rows = jnp.where(owned[:, None], projected[pick_slot], jnp.float32(0.0))
-    pick_rows = lax.psum(local_rows, ("rows", "cols"))
+    parts = lax.all_gather(local_rows, ("rows", "cols"), axis=0, tiled=False)
+    pick_rows = parts.sum(axis=0)
     pick_sq = jnp.sum(pick_rows * pick_rows, axis=1)
     own_sq = jnp.sum(projected * projected, axis=1)
     inner_prod = jnp.dot(projected, pick_rows.T, precision=lax.Precision.HIGHEST)

time: 382 us -> 366 us (0.958)
  waiting for transfers between devices: 261 us -> 225 us
  other arithmetic: 51.2 us -> 71.2 us
    psum x1 -> x0, waiting for transfers between devices: 253 us -> none  [shards(): pick_rows = lax.psum(local_rows, ('rows', 'cols'))]
    all_gather x0 -> x1, waiting for transfers between devices: none -> 217 us  [shards(): parts = lax.all_gather(local_rows, ('rows', 'cols'), axis=0, tiled=False)]
    reduce_sum x0 -> x1, other arithmetic: none -> 21 us  [shards(): pick_rows = parts.sum(axis=0)]
    ppermute x2, waiting for transfers between devices: 3.22 us -> 7.28 us  [padded_2(): lax.ppermute(lax.slice_in_dim(block, block.shape[dim] - width, None, axis...]
where the time goes in v1:
time: 366 us; the launch traced here: 365 us
  waiting for transfers between devices  225 us (61%)
  other arithmetic  71.2 us (19%)
  matrix products  26.9 us (7%)
  local copies, waits for them, and re-layouts  18 us (5%)
  between operations  13.6 us (4%)
  starting transfers between devices  10.2 us (3%)
    all_gather x1, waiting for transfers between devices, shards(): parts = lax.all_gather(local_rows, ('rows', 'cols'), axis=0, tiled=False)  217 us
    div x1, other arithmetic, window_sum(): return total / 9.0  47.2 us
    reduce_sum x1, other arithmetic, shards(): pick_rows = parts.sum(axis=0)  21 us
    dot_general x1, matrix products, shards(): projected = jnp.dot(pooled, proj_full, precision=lax.Precision.HIGHEST)  18.7 us
    unnamed x10, local copies, waits for them, and re-layouts  11.6 us
    dot_general x1, matrix products, shards(): jnp.dot(projected, pick_rows.T, precision=lax.Precision.HIGHEST)  8.2 us
  transfers between devices with their start and end apart: 5, of which 4 were waited for; matrix products, arithmetic and copies ran while one was open for 2% of the time, Pallas kernels for 0%

profile of v1, /device:TPU:2, one launch (start us, length us, event | category | flops | bytes accessed | tf_op | source)
XLA Modules:
  0.0 364.8 jit_solution(11232785804806109961)
XLA Ops:
  6.5 0.0 copy-start
  6.5 0.0 all-gather.2.cloned.1.call-start
  6.5 1.2 fusion.6
  7.8 1.9 collective-permute-start.1
  9.7 2.4 collective-permute-start
  12.1 0.7 broadcast_compare_fusion
  12.8 0.7 compare_select_fusion
  13.5 5.9 %collective-permute-done = bf16[1,128,1536]{2,1,0:T(8,128)(2,1)S(1)} collective-permute-done((bf16[1,128,1536]{2,1,0:T(8,128)(2,1)S(1)}, bf16[1,128,1536]{2,1,0:T(8,128)(2,1)S(1)}, u32[]{:S(2)}, u32[]{:S(2)}) %collective-permute-start) | collective-permute-done | bytes 393248 | tf_op jit(solution)/shard_map/ppermute | solution.py:14
  19.5 6.7 %constant_dynamic-update-slice_fusion.1 = bf16[34,128,1536]{2,1,0:T(8,128)(2,1)S(1)} fusion(bf16[34,128,1536]{2,1,0:T(8,128)(2,1)S(1)} %constant_dynamic-update-slice_fusion.2, bf16[32,128,1536]{2,1,0:T(8,128)(2,1)} %param.6), kind=kLoop, calls=%fused_computation.25 | loop fusion | bytes 25165824
  26.1 0.0 collective-permute-done.1
  26.2 0.0 copy-start.1
  26.2 4.8 %copy-done.1 = bf16[34,128,1536]{2,1,0:T(8,128)(2,1)} copy-done((bf16[34,128,1536]{2,1,0:T(8,128)(2,1)}, bf16[34,128,1536]{2,1,0:T(8,128)(2,1)S(1)}, u32[]{:S(2)}) %copy-start.1) | copy-done | bytes 13369368
  31.0 0.3 fusion.5
  31.4 1.3 collective-permute-start.3
  32.7 4.6 %collective-permute-start.2 = (bf16[34,1,1536]{2,0,1:T(8,128)(2,1)S(1)}, bf16[34,1,1536]{2,0,1:T(8,128)(2,1)S(1)}, u32[]{:S(2)}, u32[]{:S(2)}) collective-permute-start(bf16[34,1,1536]{2,0,1:T(8,128)(2,1)S(1)} %copy.20), channel_id=1, source_target_pairs={{0,1},{1,2},{2,3},{3,4},{4,5},{5,6},{6,7},{7,8},{8,9},{9,10},{10,1... | collective-permute-start | bytes 313352 | tf_op jit(solution)/shard_map/ppermute | solution.py:14
  37.3 0.9 collective-permute-done.3
  38.2 0.2 copy.23
  38.4 1.3 collective-permute-done.2
  39.7 0.2 copy.21
  39.9 47.2 %add_multiply_fusion = f32[32,128,1536]{2,1,0:T(8,128)} fusion(bf16[32,128,1536]{2,1,0:T(8,128)(2,1)} %param.6, bf16[34,128,1536]{2,1,0:T(8,128)(2,1)} %copy-done.1, bf16[34,1,1536]{2,1,0:T(2,128)(2,1)S(1)} %copy.23, bf16[34,1,1536]{2,1,0:T(2,128)(2,1)S(1)} %copy.21, bf16[1,128,1536]{2,1,0:T(8,128)(2,1)S(1)} %collective-permute-done.1, ...), kind=kLoop, calls=%fused_computation.1 | loop fusion | flops 264241152 | bytes 52113408 | tf_op jit(solution)/shard_map/div | solution.py:29
  87.1 18.7 %multiply_reduce_fusion.1 = (f32[4096]{0:T(1024)S(1)}, f32[4096,128]{0,1:T(8,128)S(1)}) fusion(f32[4096,1536]{1,0:T(8,128)} %bitcast.11, bf16[1536,128]{1,0:T(8,128)(2,1)S(1)} %copy-done), kind=kOutput, calls=%fused_computation.19 | convolution fusion | flops 9664720896 | bytes 27672576 | tf_op jit(solution)/shard_map/dot_general | solution.py:39
  105.9 1.9 copy.24
  107.7 2.6 gather_fusion
  110.3 0.8 bitcast_select_fusion
  111.2 0.0 all-gather.2.cloned.1.call-update
  111.2 0.0 copy-start.2
  111.2 0.0 copy-start.3
  111.2 216.7 %all-gather.2.cloned.1.call-done = f32[256,512,128]{2,1,0:T(8,128)} async-done(((f32[1,512,128]{2,1,0:T(8,128)}), f32[256,512,128]{2,1,0:T(8,128)}) %all-gather.2.cloned.1.call-update) | async-done | bytes 67108880 | tf_op jit(solution)/shard_map/all_gather | solution.py:41
  327.9 21.0 %reduce_sum.28 = f32[512,128]{1,0:T(8,128)S(1)} reduce(f32[256,512,128]{2,1,0:T(8,128)} %all-gather.2.cloned.1.call-done, f32[]{:T(128)} %constant.7.clone.1), dimensions={0}, to_apply=%region_1.2 | reduce | flops 16711680 | bytes 67371008 | tf_op jit(solution)/shard_map/reduce_sum | solution.py:42
  349.0 0.1 multiply_reduce_fusion.2
  349.1 8.2 %multiply_reduce_fusion = f32[4096]{0:T(1024)S(1)} fusion(f32[4096,128]{0,1:T(8,128)S(1)} %get-tuple-element.10, f32[512,128]{1,0:T(8,128)S(1)} %reduce_sum.28, f32[512]{0:T(512)S(1)} %multiply_reduce_fusion.2, f32[4096]{0:T(1024)S(1)} %get-tuple-element.9), kind=kOutput, calls=%fused_computation.18 | convolution fusion | flops 3231707136 | bytes 2394112 | tf_op jit(solution)/shard_map/dot_general | solution.py:45
  357.4 0.6 fusion.4
  (8 shorter events, 0.1 us)
Async XLA Ops:
  6.5 80.6 %copy-start = (bf16[1536,128]{1,0:T(8,128)(2,1)S(1)}, bf16[1536,128]{1,0:T(8,128)(2,1)}, u32[]{:S(2)}) copy-start(bf16[1536,128]{1,0:T(8,128)(2,1)} %param.7) | copy-start | bytes 1179652
  6.5 321.4 %all-gather.2.cloned.1.call-start = ((), (), s32[]{:S(2)}) async-start(), calls=%async_computation | async-start | bytes 67371008 | tf_op jit(solution)/shard_map/all_gather | solution.py:41
  7.8 18.4 %collective-permute-start.1 = (bf16[1,128,1536]{2,1,0:T(8,128)(2,1)S(1)}, bf16[1,128,1536]{2,1,0:T(8,128)(2,1)S(1)}, u32[]{:S(2)}, u32[]{:S(2)}) collective-permute-start(bf16[1,128,1536]{2,1,0:T(8,128)(2,1)S(1)} %get-tuple-element.7), channel_id=1, source_target_pairs={{32,0},{64,32},{96,64},{128,96},{160,128},{192,160},{224,192},{33,... | collective-permute-start | bytes 1179656 | tf_op jit(solution)/shard_map/ppermute | solution.py:17
  9.7 9.7 %collective-permute-start = (bf16[1,128,1536]{2,1,0:T(8,128)(2,1)S(1)}, bf16[1,128,1536]{2,1,0:T(8,128)(2,1)S(1)}, u32[]{:S(2)}, u32[]{:S(2)}) collective-permute-start(bf16[1,128,1536]{2,1,0:T(8,128)(2,1)S(1)} %get-tuple-element.8), channel_id=1, source_target_pairs={{0,32},{32,64},{64,96},{96,128},{128,160},{160,192},{192,224},{1,3... | collective-permute-start | bytes 1179656 | tf_op jit(solution)/shard_map/ppermute | solution.py:14
  26.2 4.8 %copy-start.1 = (bf16[34,128,1536]{2,1,0:T(8,128)(2,1)}, bf16[34,128,1536]{2,1,0:T(8,128)(2,1)S(1)}, u32[]{:S(2)}) copy-start(bf16[34,128,1536]{2,1,0:T(8,128)(2,1)S(1)} %constant_dynamic-update-slice_fusion) | copy-start | bytes 40108036
  31.4 6.8 %collective-permute-start.3 = (bf16[34,1,1536]{2,0,1:T(8,128)(2,1)S(1)}, bf16[34,1,1536]{2,0,1:T(8,128)(2,1)S(1)}, u32[]{:S(2)}, u32[]{:S(2)}) collective-permute-start(bf16[34,1,1536]{2,0,1:T(8,128)(2,1)S(1)} %copy.22), channel_id=1, source_target_pairs={{1,0},{2,1},{3,2},{4,3},{5,4},{6,5},{7,6},{8,7},{9,8},{10,9},{11,1... | collective-permute-start | bytes 313352 | tf_op jit(solution)/shard_map/ppermute | solution.py:17
  32.7 7.0 %collective-permute-start.2 = (bf16[34,1,1536]{2,0,1:T(8,128)(2,1)S(1)}, bf16[34,1,1536]{2,0,1:T(8,128)(2,1)S(1)}, u32[]{:S(2)}, u32[]{:S(2)}) collective-permute-start(bf16[34,1,1536]{2,0,1:T(8,128)(2,1)S(1)} %copy.20), channel_id=1, source_target_pairs={{0,1},{1,2},{2,3},{3,4},{4,5},{5,6},{6,7},{7,8},{8,9},{9,10},{10,1... | collective-permute-start | bytes 313352 | tf_op jit(solution)/shard_map/ppermute | solution.py:14
  111.2 246.1 %copy-start.2 = (f32[32,128]{1,0:T(8,128)S(1)}, f32[32,128]{1,0:T(8,128)}, u32[]{:S(2)}) copy-start(f32[32,128]{1,0:T(8,128)} %param.8) | copy-start | bytes 49156
  111.2 246.1 %copy-start.3 = (s32[32,128]{1,0:T(8,128)S(1)}, s32[32,128]{1,0:T(8,128)}, u32[]{:S(2)}) copy-start(s32[32,128]{1,0:T(8,128)} %param.9) | copy-start | bytes 49156
Sparse Core Ops, SparseCore 0:
  111.3 216.5 all-gather.1
